TPU v7x, 32 devices: a whole 2x2x4 slice. The times are simulated.
32 devices in a mesh: groups: 2 (over y), row: 16 (over z, x, core).
Axes of the slice: x: 2, y: 2, z: 4, core: 2. Of those that a mesh axis runs over, the one named last changes fastest.
Arguments:
- activations: bfloat16 [768, 8192], P('groups', 'row'), parts along dimension 0, may hold values from -24 to 24
- norm_gain: bfloat16 [8192], P('row'), may hold values from 0.099609375 to 1.8984375
- gate_weight: bfloat16 [8192, 28672], P(None, 'row'), may hold values from -0.0625 to 0.0625
- up_weight: bfloat16 [8192, 28672], P(None, 'row'), may hold values from -0.0625 to 0.0625
- down_weight: bfloat16 [28672, 8192], P('row'), may hold values from -0.046875 to 0.046875
Outputs:
- mlp_out: bfloat16 [768, 8192], P('groups', 'row'), parts along dimension 0
There are 2 independent parts, one for each index of `groups`. A program takes and returns all parts, laid end to end along the dimension named above; an argument that names none is the same for every part. Nothing has to cross between parts.
All inputs are finite; a program needn't handle non-finite values.
Results may differ from a plain program's by a relative error of at most 0.0065.
Values may be sent and summed in bfloat16 or wider, within the bound.
A program may use at most 192 MiB of HBM per device.

v0:
```python
import jax
import jax.numpy as jnp
from jax import lax
from jax.sharding import PartitionSpec as P

D = 8192


def per_device(activations, norm_gain, gate_weight, up_weight, down_weight):
    float_rows = activations.astype(jnp.float32)
    square_sums = lax.psum(jnp.sum(float_rows * float_rows, axis=1), "row")
    inv_scale = lax.rsqrt(square_sums / D + 1e-05)
    normed = (float_rows * inv_scale[:, None] * norm_gain.astype(jnp.float32)[None, :]).astype(
        jnp.bfloat16
    )
    shard_rows = lax.all_gather(normed, "row", axis=1, tiled=True)
    gate_proj = jnp.dot(shard_rows, gate_weight, preferred_element_type=jnp.float32)
    up_proj = jnp.dot(shard_rows, up_weight, preferred_element_type=jnp.float32)
    hidden = (jax.nn.silu(gate_proj) * up_proj).astype(jnp.bfloat16)
    reduced = lax.psum_scatter(
        lax.dot_general(
            down_weight, hidden, (((0,), (1,)), ((), ())), preferred_element_type=jnp.float32
        ),
        "row",
        scatter_dimension=0,
        tiled=True,
    )
    return reduced.T.astype(jnp.bfloat16)


def solution(mesh):
    in_specs = (P("groups", "row"), P("row"), P(None, "row"), P(None, "row"), P("row", None))
    out_specs = P("groups", "row")
    return jax.shard_map(
        per_device, mesh=mesh, in_specs=in_specs, out_specs=out_specs, check_vma=False
    )
```

profile of v0, /device:TPU:0, one launch (start us, length us, event | category | flops | bytes accessed | tf_op | source)
XLA Modules:
  0.0 305.9 jit_solution(5603079134771323414)
XLA Ops:
  6.5 0.0 all-gather.2.cloned.1.call-start
  6.5 0.7 convert_element_type.19
  7.2 1.2 fusion.1
  8.4 34.9 %psum.7 = f32[384]{0:T(512)S(1)} all-reduce(f32[384]{0:T(512)S(1)} %fusion.1), channel_id=1, replica_groups=mesh['groups'=2,'row'=16] {'row'}, use_global_device_ids=true, to_apply=%region_1.0 | all-reduce | flops 384 | bytes 3072 | tf_op jit(solution)/shard_map/psum | solution.py:11
  43.3 1.9 fusion.3
  45.2 0.0 all-gather.2.cloned.1.call-update
  45.2 0.0 reduce-scatter.2.cloned.1.call-start
  45.3 62.6 %all-gather.2.cloned.1.call-done = bf16[384,8192]{1,0:T(8,128)(2,1)} async-done(((bf16[384,512]{1,0:T(8,128)(2,1)}), bf16[384,8192]{1,0:T(8,128)(2,1)}) %all-gather.2.cloned.1.call-update) | async-done | bytes 6291472 | tf_op jit(solution)/shard_map/all_gather | solution.py:16
  107.9 0.0 copy-start
  107.9 19.6 %fusion.4 = f32[384,1792]{1,0:T(8,128)} fusion(bf16[384,8192]{1,0:T(8,128)(2,1)} %all-gather.2.cloned.1.call-done, bf16[8192,1792]{1,0:T(8,128)(2,1)} %param.7), kind=kOutput, calls=%fused_computation.10 | convolution fusion | flops 11274289152 | bytes 38404096 | tf_op jit(solution)/shard_map/dot_general | solution.py:17
  127.5 0.0 copy-done
  127.5 16.7 %fusion = bf16[384,1792]{1,0:T(8,128)(2,1)S(1)} fusion(bf16[384,8192]{1,0:T(8,128)(2,1)S(1)} %copy-done, bf16[8192,1792]{1,0:T(8,128)(2,1)} %param.8, f32[384,1792]{1,0:T(8,128)} %fusion.4), kind=kOutput, calls=%fused_computation.2 | convolution fusion | flops 11278417920 | bytes 39780352 | tf_op jit(solution)/shard_map/dot_general | solution.py:18
  144.2 19.8 %convolution_bitcast_fusion = f32[8192,384]{0,1:T(8,128)} fusion(bf16[384,1792]{1,0:T(8,128)(2,1)S(1)} %fusion, bf16[1792,8192]{1,0:T(8,128)(2,1)} %param.9), kind=kOutput, calls=%fused_computation | convolution fusion | flops 11274289152 | bytes 43319296 | tf_op jit(solution)/shard_map/dot_general | solution.py:21
  164.0 0.0 reduce-scatter.2.cloned.1.call-update
  164.0 133.1 %reduce-scatter.2.cloned.1.call-done = f32[512,384]{0,1:T(8,128)} async-done(((f32[8192,384]{0,1:T(8,128)}), f32[512,384]{0,1:T(8,128)}) %reduce-scatter.2.cloned.1.call-update) | async-done | bytes 786448 | tf_op jit(solution)/shard_map/reduce_scatter | solution.py:20
  297.1 1.9 convert_bitcast_fusion
  (1 shorter events, 0.0 us)
Async XLA Ops:
  6.5 101.4 %all-gather.2.cloned.1.call-start = ((), (), s32[]{:S(2)}) async-start(), calls=%async_computation.1 | async-start | bytes 6684672 | tf_op jit(solution)/shard_map/all_gather | solution.py:16
  45.2 251.9 %reduce-scatter.2.cloned.1.call-start = ((), (), s32[]{:S(2)}) async-start(), calls=%async_computation.2 | async-start | bytes 13369344 | tf_op jit(solution)/shard_map/reduce_scatter | solution.py:20
  107.9 19.6 %copy-start = (bf16[384,8192]{1,0:T(8,128)(2,1)S(1)}, bf16[384,8192]{1,0:T(8,128)(2,1)}, u32[]{:S(2)}) copy-start(bf16[384,8192]{1,0:T(8,128)(2,1)} %all-gather.2.cloned.1.call-done) | copy-start | bytes 18874372
Sparse Core Ops, SparseCore 0:
  45.4 62.5 all-gather.1
  164.1 132.9 reduce-scatter.1
where the time goes:
time: 306 us
  waiting for transfers between devices  196 us (64%)
  matrix products  56.1 us (18%)
  blocking collectives  34.9 us (11%)
  between operations  13.4 us (4%)
  other arithmetic  5.67 us (2%)
    reduce_scatter x1, waiting for transfers between devices, per_device(): lax.psum_scatter(lax.dot_general(down_weight, hidden, (((0,), (1,)), ((),...  133 us
    all_gather x1, waiting for transfers between devices, per_device(): shard_rows = lax.all_gather(normed, 'row', axis=1, tiled=True)  62.6 us
    psum x1, blocking collectives, per_device(): square_sums = lax.psum(jnp.sum(float_rows * float_rows, axis=1), 'row')  34.9 us
    dot_general x1, matrix products, per_device(): lax.dot_general(down_weight, hidden, (((0,), (1,)), ((), ())), preferred_...  19.8 us
    dot_general x1, matrix products, per_device(): jnp.dot(shard_rows, gate_weight, preferred_element_type=jnp.float32)  19.6 us
    dot_general x1, matrix products, per_device(): up_proj = jnp.dot(shard_rows, up_weight, preferred_element_type=jnp.float32)  16.7 us
  transfers between devices with their start and end apart: 2, of which 2 were waited for; matrix products, arithmetic and copies ran while one was open for 0% of the time, Pallas kernels for 0%

commit v1 on v0

--- a/solution.py
+++ b/solution.py
@@ -1,12 +1,22 @@
+import functools
+
 import jax
 import jax.numpy as jnp
 from jax import lax
+from jax.experimental import pallas as pl
+from jax.experimental.pallas import tpu as pltpu
 from jax.sharding import PartitionSpec as P
 
 D = 8192
-
-
-def per_device(activations, norm_gain, gate_weight, up_weight, down_weight):
+Z, X, H = 4, 2, 2
+COLS = 256
+MESH = pl.DeviceIdType.MESH
+NEAR = ((0, 1, 2, 3), (1, 0, 2, 3), (2, 1, 3, 0), (3, 2, 1, 0))
+ORDER_END = (0, 1, 4, 2, 5, 3, 6, 7)
+ORDER_MID = (0, 1, 2, 4, 3, 5, 6, 7)
+
+
+def plain(activations, norm_gain, gate_weight, up_weight, down_weight):
     float_rows = activations.astype(jnp.float32)
     square_sums = lax.psum(jnp.sum(float_rows * float_rows, axis=1), "row")
     inv_scale = lax.rsqrt(square_sums / D + 1e-05)
@@ -28,9 +38,370 @@
     return reduced.T.astype(jnp.bfloat16)
 
 
+def pick(table, index):
+    value = jnp.int32(table[0])
+    for at in range(1, len(table)):
+        value = jnp.where(index == at, jnp.int32(table[at]), value)
+    return value
+
+
+def near_z(z, k):
+    value = pick(NEAR[0], k)
+    for at in range(1, Z):
+        value = jnp.where(z == at, pick(NEAR[at], k), value)
+    return value
+
+
+def kernel(
+    act, gain, gate_w, up_w, down_w, out,
+    gathered, stats, squares, inv, xn, w_buf, acc, hidden, dw_buf,
+    core_out, core_in, x_out, x_in, z_out, z_in, total,
+    act_sem, w_sem, dw_sem, stat_send, stat_recv,
+    g_recv, g_up, g_down, g_x, g_core,
+    core_send, core_recv, x_send, x_recv, z_send, z_recv,
+):
+    n = 2 * Z * X
+    me = lax.axis_index("row")
+    c = lax.rem(me, 2)
+    x = lax.rem(me // 2, X)
+    z = me // (2 * X)
+    tokens, wide = hidden.shape
+    half = tokens // H
+    feat = gathered.shape[3]
+    steps = Z * X
+    partner = me + 1 - 2 * c
+    across = me + 2 - 4 * x
+    above = jnp.minimum(me + 2 * X, n - 1)
+    below = jnp.maximum(me - 2 * X, 0)
+
+    def remote(src, dst, send, recv, target):
+        return pltpu.make_async_remote_copy(
+            src_ref=src, dst_ref=dst, send_sem=send, recv_sem=recv,
+            device_id={"row": target}, device_id_type=MESH,
+        )
+
+    def place(s):
+        code = jnp.where(
+            (z == 0) | (z == Z - 1), pick(ORDER_END, s), pick(ORDER_MID, s)
+        )
+        in_line = code < Z
+        k = lax.rem(code, Z)
+        zz = near_z(z, k)
+        chip = zz * X + jnp.where(in_line, x, 1 - x)
+        return in_line, k, zz, chip
+
+    def weights(s):
+        _, _, _, chip = place(s)
+        rows = pl.ds(pl.multiple_of(chip * 2 * feat, 2 * feat), 2 * feat)
+        slot = lax.rem(s, 2)
+        return [
+            pltpu.make_async_copy(w.at[rows], w_buf.at[slot, i], w_sem.at[slot, i])
+            for i, w in enumerate((gate_w, up_w))
+        ]
+
+    def dest(kk):
+        k = Z - 1 - lax.rem(kk, Z)
+        zz = near_z(z, k)
+        return zz, zz * X + jnp.where(kk < Z, 1 - x, x)
+
+    def down(kk, mine):
+        _, chip = dest(kk)
+        core = jnp.where(mine == 1, c, 1 - c)
+        cols = pl.ds(pl.multiple_of((chip * 2 + core) * feat, feat), feat)
+        slot = lax.rem(kk, 2) * 2 + mine
+        return pltpu.make_async_copy(down_w.at[:, cols], dw_buf.at[slot], dw_sem.at[slot])
+
+    own = pltpu.make_async_copy(act, gathered.at[me], act_sem)
+    own.start()
+    for copy in weights(0) + weights(1):
+        copy.start()
+
+    barrier = pltpu.get_barrier_semaphore()
+    for step in range(1, n):
+        pl.semaphore_signal(
+            barrier, inc=1, device_id={"row": lax.rem(me + step, n)}, device_id_type=MESH
+        )
+
+    own.wait()
+    for h in range(H):
+        rows = gathered[me, h].astype(jnp.float32)
+        sums = jnp.sum(rows * rows, axis=1, keepdims=True)
+        squares[h * half : (h + 1) * half, :] = jnp.broadcast_to(sums, (half, 128))
+    blocks = tokens // 128
+    lines = feat // 128
+    for b in range(blocks):
+        stats[me, b : b + 1, :] = squares[b * 128 : (b + 1) * 128, :].T[0:1, :]
+    for j in range(lines):
+        stats[me, blocks + j : blocks + j + 1, :] = gain[:, j * 128 : (j + 1) * 128].astype(
+            jnp.float32
+        )
+    pl.semaphore_wait(barrier, n - 1)
+
+    def stat_copy(step):
+        return remote(
+            stats.at[me], stats.at[me], stat_send.at[step - 1], stat_recv.at[me],
+            lax.rem(me + step, n),
+        )
+
+    for step in range(1, n):
+        stat_copy(step).start()
+
+    def onward(s, h):
+        in_line, k, zz, chip = place(s)
+        chunk = chip * 2 + c
+        ref, recv = gathered.at[chunk, h], g_recv.at[chunk, h]
+        return (
+            (remote(ref, ref, g_x.at[k, h], recv, across), in_line),
+            (remote(ref, ref, g_up.at[k, h], recv, above), in_line & (zz <= z) & (z < Z - 1)),
+            (remote(ref, ref, g_down.at[k, h], recv, below), in_line & (zz >= z) & (z > 0)),
+            (remote(ref, ref, g_core.at[s, h], recv, partner), s >= 0),
+        )
+
+    def arrived(chunk, h):
+        ref = gathered.at[chunk, h]
+        pltpu.make_async_copy(ref, ref, g_recv.at[chunk, h]).wait()
+
+    def pass_on(s, h):
+        for copy, needed in onward(s, h):
+            @pl.when(needed)
+            def _():
+                copy.start()
+
+    for h in range(H):
+        pass_on(jnp.int32(0), h)
+    acc[...] = jnp.zeros_like(acc)
+    for kk in range(2):
+        for mine in range(2):
+            down(jnp.int32(kk), mine).start()
+
+    for step in range(1, n):
+        origin = lax.rem(me + step, n)
+        pltpu.make_async_copy(stats.at[origin], stats.at[origin], stat_recv.at[origin]).wait()
+    sums = stats[0]
+    for origin in range(1, n):
+        sums = sums + stats[origin]
+    scale = lax.rsqrt(sums / (n * feat) + 1e-05)
+    for b in range(blocks):
+        inv[b * 128 : (b + 1) * 128, :] = jnp.broadcast_to(scale[b : b + 1, :], (128, 128)).T
+
+    def gather_step(s, carry):
+        _, _, _, chip = place(s)
+        slot = lax.rem(s, 2)
+        for h in range(H):
+            arrived(chip * 2 + 1 - c, h)
+        for core in range(2):
+            for h in range(H):
+                rows = slice(h * half, (h + 1) * half)
+                for j in range(lines):
+                    part = gathered[chip * 2 + core, h, :, j * 128 : (j + 1) * 128]
+                    scaled = part.astype(jnp.float32) * inv[rows, :]
+                    scaled = scaled * stats[chip * 2 + core, blocks + j : blocks + j + 1, :]
+                    at = core * feat + j * 128
+                    xn[rows, at : at + 128] = scaled.astype(jnp.bfloat16)
+        for i in range(2):
+            weights(s)[i].wait()
+            acc[i] += jnp.dot(xn[...], w_buf[slot, i], preferred_element_type=jnp.float32)
+
+            @pl.when(s < steps - 2)
+            def _():
+                weights(s + 2)[i].start()
+
+            @pl.when(s < steps - 1)
+            def _():
+                _, _, _, chip_next = place(s + 1)
+                arrived(chip_next * 2 + c, i)
+                pass_on(s + 1, i)
+
+        return carry
+
+    lax.fori_loop(0, steps, gather_step, 0)
+
+    def activate(t, carry):
+        cols = pl.ds(pl.multiple_of(t * COLS, COLS), COLS)
+        gate = acc[0, :, cols]
+        hidden[:, cols] = (gate / (1.0 + jnp.exp(-gate)) * acc[1, :, cols]).astype(jnp.bfloat16)
+        return carry
+
+    lax.fori_loop(0, wide // COLS, activate, 0)
+
+    def core_copy(kk):
+        return remote(
+            core_out.at[kk], core_in.at[kk], core_send.at[kk], core_recv.at[kk], partner
+        )
+
+    def x_copy(k, h):
+        return remote(x_out.at[k, h], x_in.at[k, h], x_send.at[k, h], x_recv.at[k, h], across)
+
+    def z_copy(zz, h, side, target):
+        return remote(
+            z_out.at[zz, h], z_in.at[side, zz, h], z_send.at[zz, h], z_recv.at[side, zz, h], target
+        )
+
+    def reduce_step(kk, carry):
+        zz, _ = dest(kk)
+        k = lax.rem(kk, Z)
+        for mine in range(2):
+            down(kk, mine).wait()
+            slot = lax.rem(kk, 2) * 2 + mine
+            part = jnp.dot(hidden[...], dw_buf[slot], preferred_element_type=jnp.float32)
+            if mine:
+                total[...] = part
+            else:
+                core_out[kk] = part.astype(jnp.bfloat16)
+                core_copy(kk).start()
+
+            @pl.when(kk < steps - 2)
+            def _():
+                down(kk + 2, mine).start()
+
+        core_copy(kk).wait_recv()
+
+        @pl.when(kk < Z)
+        def _():
+            for h in range(H):
+                rows = slice(h * half, (h + 1) * half)
+                joined = total[rows, :] + core_in[kk, rows, :].astype(jnp.float32)
+                x_out[k, h] = joined.astype(jnp.bfloat16)
+                x_copy(k, h).start()
+
+        @pl.when(kk >= Z)
+        def _():
+            for h in range(H):
+                rows = slice(h * half, (h + 1) * half)
+                joined = total[rows, :] + core_in[kk, rows, :].astype(jnp.float32)
+                x_copy(k, h).wait_recv()
+                total[rows, :] = joined + x_in[k, h].astype(jnp.float32)
+
+                @pl.when((z > 0) & (zz >= z))
+                def _():
+                    z_copy(zz, h, 0, above).wait_recv()
+                    total[rows, :] += z_in[0, zz, h].astype(jnp.float32)
+
+                @pl.when((z < Z - 1) & (zz <= z))
+                def _():
+                    z_copy(zz, h, 1, below).wait_recv()
+                    total[rows, :] += z_in[1, zz, h].astype(jnp.float32)
+
+                @pl.when(zz == z)
+                def _():
+                    out[rows, :] = total[rows, :].astype(jnp.bfloat16)
+
+                @pl.when(zz != z)
+                def _():
+                    z_out[zz, h] = total[rows, :].astype(jnp.bfloat16)
+
+                @pl.when(zz > z)
+                def _():
+                    z_copy(zz, h, 0, above).start()
+
+                @pl.when(zz < z)
+                def _():
+                    z_copy(zz, h, 1, below).start()
+
+        return carry
+
+    lax.fori_loop(0, steps, reduce_step, 0)
+
+    for step in range(1, n):
+        stat_copy(step).wait_send()
+
+    def drain(s, carry):
+        for h in range(H):
+            for copy, needed in onward(s, h):
+                @pl.when(needed)
+                def _():
+                    copy.wait_send()
+        core_copy(s).wait_send()
+        return carry
+
+    lax.fori_loop(0, steps, drain, 0)
+
+    def drain_sums(k, carry):
+        for h in range(H):
+            x_copy(k, h).wait_send()
+
+            @pl.when(k != z)
+            def _():
+                z_copy(k, h, 0, above).wait_send()
+        return carry
+
+    lax.fori_loop(0, Z, drain_sums, 0)
+
+
+def fused(activations, norm_gain, gate_weight, up_weight, down_weight):
+    tokens, feat = activations.shape
+    wide = gate_weight.shape[1]
+    n, steps, half = 2 * Z * X, Z * X, tokens // H
+    bf16, f32 = jnp.bfloat16, jnp.float32
+    anywhere = pl.BlockSpec(memory_space=pl.ANY)
+    vmem = pl.BlockSpec(memory_space=pltpu.VMEM)
+    dma = pltpu.SemaphoreType.DMA
+    return pl.pallas_call(
+        kernel,
+        out_shape=jax.ShapeDtypeStruct((tokens, feat), bf16),
+        in_specs=[anywhere, vmem, anywhere, anywhere, anywhere],
+        out_specs=vmem,
+        scratch_shapes=[
+            pltpu.VMEM((n, H, half, feat), bf16),
+            pltpu.VMEM((n, 8, 128), f32),
+            pltpu.VMEM((tokens, 128), f32),
+            pltpu.VMEM((tokens, 128), f32),
+            pltpu.VMEM((tokens, 2 * feat), bf16),
+            pltpu.VMEM((2, 2, 2 * feat, wide), bf16),
+            pltpu.VMEM((2, tokens, wide), f32),
+            pltpu.VMEM((tokens, wide), bf16),
+            pltpu.VMEM((4, wide, feat), bf16),
+            pltpu.VMEM((steps, tokens, feat), bf16),
+            pltpu.VMEM((steps, tokens, feat), bf16),
+            pltpu.VMEM((Z, H, half, feat), bf16),
+            pltpu.VMEM((Z, H, half, feat), bf16),
+            pltpu.VMEM((Z, H, half, feat), bf16),
+            pltpu.VMEM((2, Z, H, half, feat), bf16),
+            pltpu.VMEM((tokens, feat), f32),
+            dma,
+            dma((2, 2)),
+            dma((4,)),
+            dma((n - 1,)),
+            dma((n,)),
+            dma((n, H)),
+            dma((Z, H)),
+            dma((Z, H)),
+            dma((Z, H)),
+            dma((steps, H)),
+            dma((steps,)),
+            dma((steps,)),
+            dma((Z, H)),
+            dma((Z, H)),
+            dma((Z, H)),
+            dma((2, Z, H)),
+        ],
+        compiler_params=pltpu.CompilerParams(
+            collective_id=0, has_side_effects=True, vmem_limit_bytes=62 * 2**20
+        ),
+    )(
+        activations.reshape(H, half, feat), norm_gain.reshape(1, feat),
+        gate_weight, up_weight, down_weight,
+    )
+
+
 def solution(mesh):
     in_specs = (P("groups", "row"), P("row"), P(None, "row"), P(None, "row"), P("row", None))
     out_specs = P("groups", "row")
+    n = mesh.shape["row"]
+
+    def per_device(activations, norm_gain, gate_weight, up_weight, down_weight):
+        tokens, feat = activations.shape
+        fits = (
+            n == 2 * Z * X
+            and tokens % 128 == 0
+            and tokens % (16 * H) == 0
+            and tokens // 128 + feat // 128 <= 8
+            and feat % 128 == 0
+            and gate_weight.shape[1] % COLS == 0
+        )
+        body = fused if fits else plain
+        return body(activations, norm_gain, gate_weight, up_weight, down_weight)
+
     return jax.shard_map(
         per_device, mesh=mesh, in_specs=in_specs, out_specs=out_specs, check_vma=False
     )

time: 306 us -> 108 us (0.35)
  waiting for transfers between devices: 196 us -> 0 us
  Pallas kernels: 0 us -> 105 us
  matrix products: 56.1 us -> 0 us
  blocking collectives: 34.9 us -> 0 us
  between operations: 13.4 us -> 0.01 us
  other arithmetic: 5.67 us -> 0 us
    reduce_scatter x1 -> x0, waiting for transfers between devices: 133 us -> none  [per_device(): lax.psum_scatter(lax.dot_general(down_weight, hidden, (((0,), (1,)), ((),...]
    pallas_call x0 -> x1, Pallas kernels: none -> 105 us  [fused(): pl.pallas_call(kernel, out_shape=jax.ShapeDtypeStruct((tokens, feat), bf1...]
    all_gather x1 -> x0, waiting for transfers between devices: 62.6 us -> none  [per_device(): shard_rows = lax.all_gather(normed, 'row', axis=1, tiled=True)]
    dot_general x3 -> x0, matrix products: 56.1 us -> none  [the longest x1 19.8 us: per_device(): lax.dot_general(down_weight, hidden, (((0,), (1,)), ((), ())), preferred_...]
    psum x1 -> x0, blocking collectives: 34.9 us -> none  [per_device(): square_sums = lax.psum(jnp.sum(float_rows * float_rows, axis=1), 'row')]
    convert_element_type x3 -> x0, other arithmetic: 4.51 us -> none  [the longest x1 1.93 us: per_device(): return reduced.T.astype(jnp.bfloat16)]
  transfers between devices with their start and end apart: 2 -> 0, of which waited for: 2 -> 0; matrix products, arithmetic and copies ran while one was open for 0% -> 0% of each run, Pallas kernels for 0% -> 0%
where the time goes in v1:
time: 108 us
  Pallas kernels  105 us (97%)
  local copies, waits for them, and re-layouts  3.03 us (3%)
    pallas_call x1, Pallas kernels, fused(): pl.pallas_call(kernel, out_shape=jax.ShapeDtypeStruct((tokens, feat), bf1...  105 us

profile of v1, /device:TPU:0, one launch (start us, length us, event | category | flops | bytes accessed | tf_op | source)
XLA Modules:
  0.0 107.7 jit_solution(16177650494500523741)
XLA Ops:
  0.0 1.3 %reshape.7.gain = bf16[1,512]{1,0:T(2,128)(2,1)} reshape(bf16[512]{0:T(512)(128)(2,1)} %param.6) | data formatting | bytes 2048 | tf_op jit(solution)/shard_map/reshape | solution.py:382
  1.3 104.6 %shard_map.55 = bf16[384,512]{1,0:T(8,128)(2,1)} custom-call(bf16[2,192,512]{2,1,0:T(8,128)(2,1)} %bitcast.1, bf16[1,512]{1,0:T(2,128)(2,1)} %reshape.7.gain, bf16[8192,1792]{1,0:T(8,128)(2,1)} %gate_w.1, bf16[8192,1792]{1,0:T(8,128)(2,1)} %up_w.1, bf16[1792,8192]{1,0:T(8,128)(2,1)} %down_w.1), custom_call_target="tpu_custom_call" | custom-call | tf_op jit(solution)/shard_map/pallas_call | solution.py:339
  105.9 1.8 %copy.7 = bf16[384,512]{1,0:T(8,128)(2,1)} copy(bf16[384,512]{1,0:T(8,128)(2,1)} %shard_map.55) | data formatting | bytes 786432

commit v2 on v1

--- a/solution.py
+++ b/solution.py
@@ -199,18 +199,19 @@
                     at = core * feat + j * 128
                     xn[rows, at : at + 128] = scaled.astype(jnp.bfloat16)
         for i in range(2):
+            @pl.when(s < steps - 1)
+            def _():
+                _, _, _, chip_next = place(s + 1)
+                for h in range(i * H // 2, (i + 1) * H // 2):
+                    arrived(chip_next * 2 + c, h)
+                    pass_on(s + 1, h)
+
             weights(s)[i].wait()
             acc[i] += jnp.dot(xn[...], w_buf[slot, i], preferred_element_type=jnp.float32)
 
             @pl.when(s < steps - 2)
             def _():
                 weights(s + 2)[i].start()
-
-            @pl.when(s < steps - 1)
-            def _():
-                _, _, _, chip_next = place(s + 1)
-                arrived(chip_next * 2 + c, i)
-                pass_on(s + 1, i)
 
         return carry
 

time: 108 us -> 103 us (0.954)
  Pallas kernels: 105 us -> 99.8 us
    pallas_call x1, Pallas kernels: 105 us -> 99.8 us  [fused(): pl.pallas_call(kernel, out_shape=jax.ShapeDtypeStruct((tokens, feat), bf1...]
where the time goes in v2:
time: 103 us
  Pallas kernels  99.8 us (97%)
  local copies, waits for them, and re-layouts  3.03 us (3%)
    pallas_call x1, Pallas kernels, fused(): pl.pallas_call(kernel, out_shape=jax.ShapeDtypeStruct((tokens, feat), bf1...  99.8 us

profile of v2, /device:TPU:0, one launch (start us, length us, event | category | flops | bytes accessed | tf_op | source)
XLA Modules:
  0.0 102.8 jit_solution(18053454668768816967)
XLA Ops:
  0.0 1.3 %reshape.7.gain = bf16[1,512]{1,0:T(2,128)(2,1)} reshape(bf16[512]{0:T(512)(128)(2,1)} %param.6) | data formatting | bytes 2048 | tf_op jit(solution)/shard_map/reshape | solution.py:383
  1.3 99.8 %shard_map.55 = bf16[384,512]{1,0:T(8,128)(2,1)} custom-call(bf16[2,192,512]{2,1,0:T(8,128)(2,1)} %bitcast.1, bf16[1,512]{1,0:T(2,128)(2,1)} %reshape.7.gain, bf16[8192,1792]{1,0:T(8,128)(2,1)} %gate_w.1, bf16[8192,1792]{1,0:T(8,128)(2,1)} %up_w.1, bf16[1792,8192]{1,0:T(8,128)(2,1)} %down_w.1), custom_call_target="tpu_custom_call" | custom-call | tf_op jit(solution)/shard_map/pallas_call | solution.py:340
  101.1 1.8 %copy.7 = bf16[384,512]{1,0:T(8,128)(2,1)} copy(bf16[384,512]{1,0:T(8,128)(2,1)} %shard_map.55) | data formatting | bytes 786432
